TPU v7x, 128 devices: a whole 4x4x4 slice. The times are simulated.
128 devices in a mesh: grp: 8 (over y_lo, z), dev: 16 (over y_hi, x, core).
Axes of the slice: x: 4, y: 4 (y_hi: 2, y_lo: 2; y = y_hi * 2 + y_lo), z: 4, core: 2. Of those that a mesh axis runs over, the one named last changes fastest.
Arguments:
- queries: bfloat16 [131072, 2048], P(('grp', 'dev')), may hold values from -48 to 48
- key_rows: bfloat16 [131072, 2048], P(('grp', 'dev')), may hold values from -6 to 6
- value_rows: bfloat16 [131072, 2048], P(('grp', 'dev')), may hold values from -6 to 6
Outputs:
- attended: bfloat16 [131072, 2048], P(('grp', 'dev'))
All inputs are finite; a program needn't handle non-finite values.
Results may differ from a plain program's by a relative error of at most 0.0026.
Values may be sent and summed in bfloat16 or wider, within the bound.
A program may use at most 256 MiB of HBM per device.

v0:
```python
import math
import jax
import jax.numpy as jnp
import numpy as np
from jax import lax
from jax.sharding import PartitionSpec as P

H = 16


def attend(query_rows, key_part, value_part):
    score_scale = 1.0 / math.sqrt(query_rows.shape[-1])
    scores = (
        jnp.einsum("qhe,khe->hqk", query_rows, key_part, preferred_element_type=jnp.float32)
        * score_scale
    )
    maxima = jnp.max(scores, axis=2)
    weights = jnp.exp(scores - maxima[:, :, None])
    totals = jnp.sum(weights, axis=2)
    summed = jnp.einsum(
        "hqk,khe->qhe", weights.astype(jnp.bfloat16), value_part, preferred_element_type=jnp.float32
    )
    return (maxima.T, totals.T, summed)


def start_state(query_rows):
    row_count, head_count, head_width = query_rows.shape
    return (
        jnp.full((row_count, head_count), -jnp.inf, jnp.float32),
        jnp.zeros((row_count, head_count), jnp.float32),
        jnp.zeros((row_count, head_count, head_width), jnp.float32),
    )


def folder(query_rows, state_now, shard_piece):
    score_scale = 1.0 / math.sqrt(query_rows.shape[-1])
    maxima, totals, summed = state_now
    key_part, value_part = shard_piece
    scores = (
        jnp.einsum("qhe,khe->hqk", query_rows, key_part, preferred_element_type=jnp.float32)
        * score_scale
    )
    raised = jnp.maximum(maxima, jnp.max(scores, axis=2).T)
    weights = jnp.exp(scores - raised.T[:, :, None])
    shrink = jnp.exp(maxima - raised)
    totals = totals * shrink + jnp.sum(weights, axis=2).T
    summed = summed * shrink[:, :, None] + jnp.einsum(
        "hqk,khe->qhe", weights.astype(jnp.bfloat16), value_part, preferred_element_type=jnp.float32
    )
    return (raised, totals, summed)


def picked_rows(source, dilation):
    head_ids = np.arange(source.shape[1])
    shaped = source.reshape(source.shape[0] // dilation, dilation, source.shape[1], source.shape[2])
    return shaped[:, head_ids % dilation, head_ids, :]


def gap_between(maxima, totals, summed, dilation):
    head_count = maxima.shape[1]
    select_mask = jnp.asarray(
        np.arange(dilation)[:, None] == (np.arange(head_count) % dilation)[None, :]
    )
    full_max = jnp.where(select_mask[None], maxima[:, None, :], -jnp.inf).reshape(-1, head_count)
    full_tot = jnp.where(select_mask[None], totals[:, None, :], 0.0).reshape(-1, head_count)
    full_sum = jnp.where(select_mask[None, :, :, None], summed[:, None], 0.0).reshape(
        -1, head_count, summed.shape[2]
    )
    return (full_max, full_tot, full_sum)


def combine(branch_list):
    highest = branch_list[0][0]
    for branch in branch_list[1:]:
        highest = jnp.maximum(highest, branch[0])
    numerator = jnp.zeros_like(branch_list[0][2])
    denominator = jnp.zeros_like(branch_list[0][1])
    for branch in branch_list:
        factor = jnp.exp(branch[0] - highest)
        denominator = denominator + branch[1] * factor
        numerator = numerator + branch[2] * factor[:, :, None]
    return numerator / denominator[:, :, None]


def body(queries, key_rows, value_rows):
    tok_rows = queries.shape[0]
    head_width = queries.shape[1] // H
    processor_count = lax.axis_size("dev")
    group_number = lax.axis_size("grp")
    global_dilation = processor_count * group_number
    query_per_head = queries.reshape(tok_rows, H, head_width)
    key_per_head = key_rows.reshape(tok_rows, H, head_width)
    value_per_head = value_rows.reshape(tok_rows, H, head_width)
    block_rows = min(512, tok_rows)
    query_blocks = query_per_head.reshape(tok_rows // block_rows, block_rows, H, head_width)
    local_max, local_tot, local_sum = lax.map(
        lambda chosen: attend(chosen, key_per_head, value_per_head), query_blocks
    )
    local_part = (
        local_max.reshape(tok_rows, H),
        local_tot.reshape(tok_rows, H),
        local_sum.reshape(tok_rows, H, head_width),
    )
    group_query = picked_rows(query_per_head, processor_count)
    group_key = picked_rows(key_per_head, processor_count)
    group_value = picked_rows(value_per_head, processor_count)
    global_query = picked_rows(query_per_head, global_dilation)
    global_key = picked_rows(key_per_head, global_dilation)
    global_value = picked_rows(value_per_head, global_dilation)
    global_portion = folder(
        global_query,
        start_state(global_query),
        (
            lax.all_gather(global_key, ("grp", "dev"), axis=0, tiled=True),
            lax.all_gather(global_value, ("grp", "dev"), axis=0, tiled=True),
        ),
    )
    group_portion = folder(
        group_query,
        start_state(group_query),
        (
            lax.all_gather(group_key, "dev", axis=0, tiled=True),
            lax.all_gather(group_value, "dev", axis=0, tiled=True),
        ),
    )
    result = combine(
        [
            local_part,
            gap_between(group_portion[0], group_portion[1], group_portion[2], processor_count),
            gap_between(global_portion[0], global_portion[1], global_portion[2], global_dilation),
        ]
    )
    return result.reshape(tok_rows, H * head_width).astype(jnp.bfloat16)


def solution(mesh):
    in_specs = (P(("grp", "dev"), None), P(("grp", "dev"), None), P(("grp", "dev"), None))
    out_specs = P(("grp", "dev"), None)
    return jax.shard_map(body, mesh=mesh, in_specs=in_specs, out_specs=out_specs, check_vma=False)
```

profile of v0, /device:TPU:1, one launch (start us, length us, event | category | flops | bytes accessed | tf_op | source)
XLA Modules:
  0.0 651.3 jit_solution(3880444532441547648)
XLA Ops:
  12.2 4.7 copy.61
  25.9 4.7 copy.66
  34.4 9.0 %copy.63 = bf16[8,128,16,128]{3,0,2,1:T(8,128)(2,1)} copy(bf16[8,128,16,128]{3,2,1,0:T(8,128)(2,1)} %bitcast.202) | data formatting | bytes 8388608 | tf_op jit(solution)/shard_map/reshape;reshape | solution.py:55
  47.1 9.1 %copy.70 = bf16[8,128,16,128]{3,0,2,1:T(8,128)(2,1)} copy(bf16[8,128,16,128]{3,2,1,0:T(8,128)(2,1)} %bitcast.200) | data formatting | bytes 8388608 | tf_op jit(solution)/shard_map/reshape;reshape | solution.py:55
  59.6 6.4 copy.53
  66.1 6.4 copy.54
  72.5 5.6 copy.84
  78.1 6.4 copy.56
  84.5 6.4 copy.57
  90.9 115.2 %while.14 = (s32[]{:T(128)}, f32[2,512,16]{1,0,2:T(2,128)S(1)}, f32[2,512,16]{1,0,2:T(2,128)S(1)}, f32[2,512,16,128]{3,2,1,0:T(8,128)}, bf16[2,512,16,128]{3,2,1...) while((s32[]{:T(128)}, f32[2,512,16]{1,0,2:T(2,128)S(1)}, ...), condition=%wide.region_3.4_spmd, body=%wide.region_0.3_spmd.sunk | while | flops 4362059776 | bytes 145096848 | solution.py:96
  94.8 14.8 %multiply_reduce_fusion.3 = (f32[16,512]{1,0:T(8,128)S(1)}, f32[16,512,1024]{2,1,0:T(8,128)}) fusion(bf16[1024,16,128]{2,0,1:T(8,128)(2,1)S(1)} %copy-done, bf16[1,512,16,128]{3,2,1,0:T(8,128)(2,1)} %constant_dynamic-slice_fusion.2), kind=kOutput, calls=%fused_computation.7.clone.1 | convolution fusion | flops 2164252672 | bytes 39878656 | tf_op jit(solution)/shard_map/while/body/eval_jaxpr/qhe,khe->hqk/dot_general | solution.py:14
  109.8 14.4 %fusion.60 = f32[16,512]{1,0:T(8,128)S(1)} fusion(f32[16,512,1024]{2,1,0:T(8,128)} %get-tuple-element.135, f32[16,512]{1,0:T(8,128)S(1)} %get-tuple-element.134), kind=kLoop, calls=%fused_computation.9.clone.1 | loop fusion | flops 25157632 | bytes 33619968 | tf_op jit(solution)/shard_map/while/body/eval_jaxpr/reduce_sum | solution.py:19
  124.5 17.8 %fusion.61 = f32[1,512,16,128]{3,1,2,0:T(8,128)} fusion(bf16[1024,16,128]{2,0,1:T(8,128)(2,1)} %get-tuple-element.160, f32[16,512,1024]{2,1,0:T(8,128)} %get-tuple-element.135, f32[16,512]{1,0:T(8,128)S(1)} %get-tuple-element.134), kind=kOutput, calls=%fused_computation.14.clone.1 | convolution fusion | flops 2172649472 | bytes 41975808 | tf_op jit(solution)/shard_map/while/body/eval_jaxpr/hqk,khe->qhe/dot_general | solution.py:20
  142.3 6.7 %copy_dynamic-update-slice_fusion.2 = f32[2,512,16,128]{3,2,1,0:T(8,128)} fusion(f32[2,512,16,128]{3,2,1,0:T(8,128)} %get-tuple-element.148, s32[]{:T(128)S(6)} %copy.162, f32[1,512,16,128]{3,1,2,0:T(8,128)} %fusion.61), kind=kLoop, calls=%fused_computation.13.clone.1 | loop fusion | bytes 8388612 | tf_op jit(solution)/shard_map/while/body/jit(dynamic_update_index_in_dim)/dynamic_update_slice | solution.py:96
  152.4 14.8 %multiply_reduce_fusion.3 = (f32[16,512]{1,0:T(8,128)S(1)}, f32[16,512,1024]{2,1,0:T(8,128)}) fusion(bf16[1024,16,128]{2,0,1:T(8,128)(2,1)S(1)} %copy-done, bf16[1,512,16,128]{3,2,1,0:T(8,128)(2,1)} %constant_dynamic-slice_fusion.2), kind=kOutput, calls=%fused_computation.7.clone.1 | convolution fusion | flops 2164252672 | bytes 39878656 | tf_op jit(solution)/shard_map/while/body/eval_jaxpr/qhe,khe->hqk/dot_general | solution.py:14
  167.4 14.3 %fusion.60 = f32[16,512]{1,0:T(8,128)S(1)} fusion(f32[16,512,1024]{2,1,0:T(8,128)} %get-tuple-element.135, f32[16,512]{1,0:T(8,128)S(1)} %get-tuple-element.134), kind=kLoop, calls=%fused_computation.9.clone.1 | loop fusion | flops 25157632 | bytes 33619968 | tf_op jit(solution)/shard_map/while/body/eval_jaxpr/reduce_sum | solution.py:19
  182.0 17.4 %fusion.61 = f32[1,512,16,128]{3,1,2,0:T(8,128)} fusion(bf16[1024,16,128]{2,0,1:T(8,128)(2,1)} %get-tuple-element.160, f32[16,512,1024]{2,1,0:T(8,128)} %get-tuple-element.135, f32[16,512]{1,0:T(8,128)S(1)} %get-tuple-element.134), kind=kOutput, calls=%fused_computation.14.clone.1 | convolution fusion | flops 2172649472 | bytes 41975808 | tf_op jit(solution)/shard_map/while/body/eval_jaxpr/hqk,khe->qhe/dot_general | solution.py:20
  199.4 6.6 %copy_dynamic-update-slice_fusion.2 = f32[2,512,16,128]{3,2,1,0:T(8,128)} fusion(f32[2,512,16,128]{3,2,1,0:T(8,128)} %get-tuple-element.148, s32[]{:T(128)S(6)} %copy.162, f32[1,512,16,128]{3,1,2,0:T(8,128)} %fusion.61), kind=kLoop, calls=%fused_computation.13.clone.1 | loop fusion | bytes 8388612 | tf_op jit(solution)/shard_map/while/body/jit(dynamic_update_index_in_dim)/dynamic_update_slice | solution.py:96
  206.1 9.0 %copy.62 = bf16[8,128,16,128]{3,0,2,1:T(8,128)(2,1)} copy(bf16[8,128,16,128]{3,2,1,0:T(8,128)(2,1)} %bitcast.197) | data formatting | bytes 8388608 | tf_op jit(solution)/shard_map/reshape;reshape | solution.py:55
  218.4 6.9 %copy.60 = bf16[64,16,16,128]{3,0,2,1:T(8,128)(2,1)} copy(bf16[64,16,16,128]{3,2,1,0:T(8,128)(2,1)} %bitcast.198) | data formatting | bytes 8388608 | tf_op jit(solution)/shard_map/reshape;reshape | solution.py:55
  228.7 3.9 multiply_reduce_fusion.1
  236.4 4.8 fusion.23
  241.6 102.9 %all-gather.7.cloned.1.call-done = bf16[1024,16,128]{2,0,1:T(8,128)(2,1)} async-done(((bf16[8,16,128]{2,0,1:T(8,128)(2,1)}), bf16[1024,16,128]{2,0,1:T(8,128)(2,1)}) %all-gather.7.cloned.1.call-update) | async-done | bytes 4194320 | tf_op jit(solution)/shard_map/all_gather | solution.py:114
  348.9 201.5 %all-gather.11.cloned.1.call-done = bf16[1024,16,128]{2,0,1:T(8,128)(2,1)} async-done(((bf16[8,16,128]{2,0,1:T(8,128)(2,1)}), bf16[1024,16,128]{2,0,1:T(8,128)(2,1)}) %all-gather.11.cloned.1.call-update) | async-done | bytes 4194320 | tf_op jit(solution)/shard_map/all_gather | solution.py:115
  553.7 5.9 div.11
  559.7 6.0 mul.91
  569.5 6.0 mul.87
  575.5 3.9 broadcast_in_dim.225
  579.4 5.8 mul.83
  585.2 6.9 %broadcast_in_dim.228 = pred[1024,16,128]{2,1,0:T(8,128)(4,1)S(1)} broadcast(pred[1024,16]{1,0:T(8,128)(4,1)S(1)} %copy.69), dimensions={0,1} | broadcast | bytes 2113536 | tf_op jit(solution)/shard_map/jit(_where)/broadcast_in_dim | solution.py:66
  592.1 6.9 %broadcast_in_dim.219 = pred[1024,16,128]{2,1,0:T(8,128)(4,1)S(1)} broadcast(pred[1024,16]{1,0:T(8,128)(4,1)S(1)} %copy.65), dimensions={0,1} | broadcast | bytes 2113536 | tf_op jit(solution)/shard_map/jit(_where)/broadcast_in_dim | solution.py:66
  599.0 45.3 %fusion.11 = bf16[1024,2048]{1,0:T(8,128)(2,1)} fusion(f32[128,8,16,128]{3,2,1,0:T(8,128)} %bitcast.203, f32[128,8,16,128]{3,2,1,0:T(8,128)} %bitcast.204, f32[128,8,16,128]{3,2,1,0:T(8,128)} %bitcast.205, f32[128,8,16,128]{3,2,1,0:T(8,128)} %bitcast.206, f32[128,8,16,128]{3,2,1,0:T(8,128)} %bitcast.207, f32[128,8,16,128]{3,2,1,0:T(8,128)} %bitcast.208, ...), kind=kLoop, calls=%fused_computation.20 | loop fusion | flops 18874368 | bytes 67108864 | tf_op jit(solution)/shard_map/convert_element_type | solution.py:133
  (83 shorter events, 55.6 us)
Async XLA Ops:
  6.5 222.2 %all-gather.5.cloned.1.call-start = ((), (), s32[]{:S(2)}) async-start(), calls=%async_computation | async-start | bytes 4456448 | tf_op jit(solution)/shard_map/all_gather | solution.py:122
  6.5 24.1 %copy-start.4 = (s32[16]{0:T(128)}, s32[16]{0:T(128)S(1)}, u32[]{:S(2)}) copy-start(s32[16]{0:T(128)S(1)} %fusion.40) | copy-start | bytes 196
  10.1 2.0 copy-start.3
  20.3 216.1 %all-gather.9.cloned.1.call-start = ((), (), s32[]{:S(2)}) async-start(), calls=%async_computation.2 | async-start | bytes 4456448 | tf_op jit(solution)/shard_map/all_gather | solution.py:123
  24.0 2.0 copy-start.2
  34.1 310.4 %all-gather.7.cloned.1.call-start = ((), (), s32[]{:S(2)}) async-start(), calls=%async_computation.1 | async-start | bytes 4227072 | tf_op jit(solution)/shard_map/all_gather | solution.py:114
  43.4 12.8 %copy-start.6 = (s32[16]{0:T(128)}, s32[16]{0:T(128)S(1)}, u32[]{:S(2)}) copy-start(s32[16]{0:T(128)S(1)} %fusion.42) | copy-start | bytes 196
  46.8 503.6 %all-gather.11.cloned.1.call-start = ((), (), s32[]{:S(2)}) async-start(), calls=%async_computation.3 | async-start | bytes 4227072 | tf_op jit(solution)/shard_map/all_gather | solution.py:115
  91.3 3.5 copy-start
  149.0 3.5 copy-start
  206.1 9.1 %copy-start.7 = (s32[16]{0:T(128)S(1)}, s32[16]{0:T(128)}, u32[]{:S(2)}) copy-start(s32[16]{0:T(128)} %copy-done.6) | copy-start | bytes 196
  206.1 11.9 %copy-start.8 = (pred[16,16]{0,1:T(8,128)(4,1)S(1)}, pred[16,16]{0,1:T(8,128)(4,1)}, u32[]{:S(2)}) copy-start(pred[16,16]{0,1:T(8,128)(4,1)} %constant.15.clone) | copy-start | bytes 772
  218.3 6.9 %copy-start.5 = (s32[16]{0:T(128)S(1)}, s32[16]{0:T(128)}, u32[]{:S(2)}) copy-start(s32[16]{0:T(128)} %copy-done.4) | copy-start | bytes 196
  218.4 9.7 %copy-start.9 = (pred[128,16]{0,1:T(8,128)(4,1)S(1)}, pred[128,16]{0,1:T(8,128)(4,1)}, u32[]{:S(2)}) copy-start(pred[128,16]{0,1:T(8,128)(4,1)} %constant.17.clone) | copy-start | bytes 6148
  232.5 2.0 copy-start.1
Sparse Core Ops, SparseCore 0:
  20.4 59.6 all-gather.4
  82.6 54.8 all-gather.8
  139.1 205.3 all-gather.6
  346.0 204.3 all-gather.10
where the time goes:
time: 658 us; the launch traced here: 651 us
  waiting for transfers between devices  305 us (46%)
  local copies, waits for them, and re-layouts  177 us (27%)
  matrix products  79.8 us (12%)
  other arithmetic  75.2 us (11%)
  between operations  13.9 us (2%)
    all_gather x1, waiting for transfers between devices, body(): lax.all_gather(global_value, ('grp', 'dev'), axis=0, tiled=True)  202 us
    all_gather x1, waiting for transfers between devices, body(): lax.all_gather(global_key, ('grp', 'dev'), axis=0, tiled=True)  103 us
    convert_element_type x1, other arithmetic, body(): return result.reshape(tok_rows, H * head_width).astype(jnp.bfloat16)  45.3 us
    another operation x6, local copies, waits for them, and re-layouts, picked_rows(): source.reshape(source.shape[0] // dilation, dilation, source.shape[1], so...  43.3 us
    dot_general x2, matrix products, attend(): jnp.einsum('hqk,khe->qhe', weights.astype(jnp.bfloat16), value_part, pref...  35.2 us
    unnamed x26, local copies, waits for them, and re-layouts  31.7 us
    dot_general x2, matrix products, attend(): jnp.einsum('qhe,khe->hqk', query_rows, key_part, preferred_element_type=j...  29.6 us
    reduce_sum x2, other arithmetic, attend(): totals = jnp.sum(weights, axis=2)  28.8 us
  transfers between devices with their start and end apart: 4, of which 2 were waited for; matrix products, arithmetic and copies ran while one was open for 34% of the time, Pallas kernels for 0%

commit v1 on v0

--- a/solution.py
+++ b/solution.py
@@ -1,3 +1,4 @@
+import functools
 import math
 import jax
 import jax.numpy as jnp
@@ -6,6 +7,19 @@
 from jax.sharding import PartitionSpec as P
 
 H = 16
+
+
+def reach_the_hubs(xx, row_dim):
+    column = []
+    for _ in range(lax.axis_size(("grp", "dev"))):
+        column.append(xx)
+    d_next = jnp.stack(column)
+    heard = lax.all_to_all(d_next, axis_name=("grp", "dev"), split_axis=0, concat_axis=0)
+    all_values = jnp.concatenate(heard, row_dim)
+    return all_values
+
+
+post_flows = functools.partial(reach_the_hubs, row_dim=0)
 
 
 def attend(query_rows, key_part, value_part):
@@ -110,10 +124,7 @@
     global_portion = folder(
         global_query,
         start_state(global_query),
-        (
-            lax.all_gather(global_key, ("grp", "dev"), axis=0, tiled=True),
-            lax.all_gather(global_value, ("grp", "dev"), axis=0, tiled=True),
-        ),
+        (lax.all_gather(global_key, ("grp", "dev"), axis=0, tiled=True), post_flows(global_value)),
     )
     group_portion = folder(
         group_query,

time: 658 us -> 495 us (0.75)
  waiting for transfers between devices: 305 us -> 129 us
  starting transfers between devices: 0.59 us -> 12.6 us
    all_gather x1 -> x0, waiting for transfers between devices: 202 us -> none  [body(): lax.all_gather(global_value, ('grp', 'dev'), axis=0, tiled=True)]
    all_gather x1, waiting for transfers between devices: 103 us -> 129 us  [body(): lax.all_gather(global_key, ('grp', 'dev'), axis=0, tiled=True)]
    all_to_all x0 -> x1, starting transfers between devices: none -> 12.1 us  [reach_the_hubs(): lax.all_to_all(d_next, axis_name=('grp', 'dev'), split_axis=0, concat_axi...]
  transfers between devices with their start and end apart: 4 -> 4, of which waited for: 2 -> 1; matrix products, arithmetic and copies ran while one was open for 34% -> 45% of each run, Pallas kernels for 0% -> 0%
where the time goes in v1:
time: 495 us; the launch traced here: 490 us
  local copies, waits for them, and re-layouts  179 us (36%)
  waiting for transfers between devices  129 us (26%)
  matrix products  79.6 us (16%)
  other arithmetic  75.2 us (15%)
  between operations  13.9 us (3%)
  starting transfers between devices  12.6 us (3%)
    all_gather x1, waiting for transfers between devices, body(): lax.all_gather(global_key, ('grp', 'dev'), axis=0, tiled=True)  129 us
    convert_element_type x1, other arithmetic, body(): return result.reshape(tok_rows, H * head_width).astype(jnp.bfloat16)  45.3 us
    another operation x6, local copies, waits for them, and re-layouts, picked_rows(): source.reshape(source.shape[0] // dilation, dilation, source.shape[1], so...  43.3 us
    dot_general x2, matrix products, attend(): jnp.einsum('hqk,khe->qhe', weights.astype(jnp.bfloat16), value_part, pref...  34.7 us
    unnamed x26, local copies, waits for them, and re-layouts  31.6 us
    dot_general x2, matrix products, attend(): jnp.einsum('qhe,khe->hqk', query_rows, key_part, preferred_element_type=j...  29.6 us
    reduce_sum x2, other arithmetic, attend(): totals = jnp.sum(weights, axis=2)  28.7 us
    broadcast_in_dim x4, local copies, waits for them, and re-layouts, gap_between(): jnp.where(select_mask[None, :, :, None], summed[:, None], 0.0)  21.5 us
  transfers between devices with their start and end apart: 4, of which 1 were waited for; matrix products, arithmetic and copies ran while one was open for 45% of the time, Pallas kernels for 0%

profile of v1, /device:TPU:1, one launch (start us, length us, event | category | flops | bytes accessed | tf_op | source)
XLA Modules:
  0.0 489.7 jit_solution(1338081896155030058)
XLA Ops:
  12.2 4.6 copy.84
  26.1 4.7 copy.89
  34.3 9.1 %copy.93 = bf16[8,128,16,128]{3,0,2,1:T(8,128)(2,1)} copy(bf16[8,128,16,128]{3,2,1,0:T(8,128)(2,1)} %bitcast.208) | data formatting | bytes 8388608 | tf_op jit(solution)/shard_map/reshape;reshape | solution.py:69
  49.2 12.1 %all-to-all-start = ((bf16[128,8,16,128]{3,1,2,0:T(8,128)(2,1)}), bf16[128,8,16,128]{3,1,2,0:T(8,128)(2,1)}, u32[]{:S(2)}, u32[]{:S(2)}) async-start(bf16[128,8,16,128]{3,1,2,0:T(8,128)(2,1)} %stack.2), calls=%async_computation | async-start | bytes 8388608 | tf_op jit(solution)/shard_map/all_to_all | solution.py:17
  61.6 9.0 %copy.86 = bf16[8,128,16,128]{3,0,2,1:T(8,128)(2,1)} copy(bf16[8,128,16,128]{3,2,1,0:T(8,128)(2,1)} %bitcast.206) | data formatting | bytes 8388608 | tf_op jit(solution)/shard_map/reshape;reshape | solution.py:69
  74.1 6.4 %copy.76 = bf16[1024,2048]{0,1:T(8,128)(2,1)} copy(bf16[1024,2048]{1,0:T(8,128)(2,1)} %param.32) | data formatting | bytes 8388608 | tf_op args[1]
  80.5 6.4 %copy.77 = bf16[1024,2048]{0,1:T(8,128)(2,1)} copy(bf16[1024,2048]{1,0:T(8,128)(2,1)} %param.33) | data formatting | bytes 8388608 | tf_op args[2]
  86.9 5.6 %copy.108 = bf16[128,8,16,128]{3,2,1,0:T(8,128)(2,1)} copy(bf16[128,8,16,128]{3,1,2,0:T(8,128)(2,1)} %bitcast.223) | data formatting | bytes 8388608
  92.5 6.4 %copy.79 = bf16[1024,16,128]{2,0,1:T(8,128)(2,1)} copy(bf16[1024,16,128]{0,2,1:T(8,128)(2,1)} %bitcast.218) | data formatting | bytes 8388608 | tf_op jit(solution)/shard_map/while | solution.py:110
  98.9 6.4 %copy.80 = bf16[1024,16,128]{2,0,1:T(8,128)(2,1)} copy(bf16[1024,16,128]{0,2,1:T(8,128)(2,1)} %bitcast.217) | data formatting | bytes 8388608 | tf_op jit(solution)/shard_map/while | solution.py:110
  105.3 114.6 %while.14 = (s32[]{:T(128)}, f32[2,512,16]{1,0,2:T(2,128)S(1)}, f32[2,512,16]{1,0,2:T(2,128)S(1)}, f32[2,512,16,128]{3,2,1,0:T(8,128)}, bf16[2,512,16,128]{3,2,1...) while((s32[]{:T(128)}, f32[2,512,16]{1,0,2:T(2,128)S(1)}, ...), condition=%wide.region_3.4_spmd, body=%wide.region_0.3_spmd.sunk | while | flops 4362059776 | bytes 145096848 | solution.py:110
  109.2 14.7 %multiply_reduce_fusion.3 = (f32[16,512]{1,0:T(8,128)S(1)}, f32[16,512,1024]{2,1,0:T(8,128)}) fusion(bf16[1024,16,128]{2,0,1:T(8,128)(2,1)S(1)} %copy-done, bf16[1,512,16,128]{3,2,1,0:T(8,128)(2,1)} %constant_dynamic-slice_fusion.2), kind=kOutput, calls=%fused_computation.7.clone.1 | convolution fusion | flops 2164252672 | bytes 39878656 | tf_op jit(solution)/shard_map/while/body/eval_jaxpr/qhe,khe->hqk/dot_general | solution.py:28
  124.2 14.4 %fusion.67 = f32[16,512]{1,0:T(8,128)S(1)} fusion(f32[16,512,1024]{2,1,0:T(8,128)} %get-tuple-element.142, f32[16,512]{1,0:T(8,128)S(1)} %get-tuple-element.141), kind=kLoop, calls=%fused_computation.9.clone.1 | loop fusion | flops 25157632 | bytes 33619968 | tf_op jit(solution)/shard_map/while/body/eval_jaxpr/reduce_sum | solution.py:33
  138.8 17.3 %fusion.68 = f32[1,512,16,128]{3,1,2,0:T(8,128)} fusion(bf16[1024,16,128]{2,0,1:T(8,128)(2,1)} %get-tuple-element.167, f32[16,512,1024]{2,1,0:T(8,128)} %get-tuple-element.142, f32[16,512]{1,0:T(8,128)S(1)} %get-tuple-element.141), kind=kOutput, calls=%fused_computation.14.clone.1 | convolution fusion | flops 2172649472 | bytes 41975808 | tf_op jit(solution)/shard_map/while/body/eval_jaxpr/hqk,khe->qhe/dot_general | solution.py:34
  156.1 6.7 %copy_dynamic-update-slice_fusion.2 = f32[2,512,16,128]{3,2,1,0:T(8,128)} fusion(f32[2,512,16,128]{3,2,1,0:T(8,128)} %get-tuple-element.155, s32[]{:T(128)S(6)} %copy.194, f32[1,512,16,128]{3,1,2,0:T(8,128)} %fusion.68), kind=kLoop, calls=%fused_computation.13.clone.1 | loop fusion | bytes 8388612 | tf_op jit(solution)/shard_map/while/body/jit(dynamic_update_index_in_dim)/dynamic_update_slice | solution.py:110
  166.2 14.9 %multiply_reduce_fusion.3 = (f32[16,512]{1,0:T(8,128)S(1)}, f32[16,512,1024]{2,1,0:T(8,128)}) fusion(bf16[1024,16,128]{2,0,1:T(8,128)(2,1)S(1)} %copy-done, bf16[1,512,16,128]{3,2,1,0:T(8,128)(2,1)} %constant_dynamic-slice_fusion.2), kind=kOutput, calls=%fused_computation.7.clone.1 | convolution fusion | flops 2164252672 | bytes 39878656 | tf_op jit(solution)/shard_map/while/body/eval_jaxpr/qhe,khe->hqk/dot_general | solution.py:28
  181.3 14.3 %fusion.67 = f32[16,512]{1,0:T(8,128)S(1)} fusion(f32[16,512,1024]{2,1,0:T(8,128)} %get-tuple-element.142, f32[16,512]{1,0:T(8,128)S(1)} %get-tuple-element.141), kind=kLoop, calls=%fused_computation.9.clone.1 | loop fusion | flops 25157632 | bytes 33619968 | tf_op jit(solution)/shard_map/while/body/eval_jaxpr/reduce_sum | solution.py:33
  195.8 17.4 %fusion.68 = f32[1,512,16,128]{3,1,2,0:T(8,128)} fusion(bf16[1024,16,128]{2,0,1:T(8,128)(2,1)} %get-tuple-element.167, f32[16,512,1024]{2,1,0:T(8,128)} %get-tuple-element.142, f32[16,512]{1,0:T(8,128)S(1)} %get-tuple-element.141), kind=kOutput, calls=%fused_computation.14.clone.1 | convolution fusion | flops 2172649472 | bytes 41975808 | tf_op jit(solution)/shard_map/while/body/eval_jaxpr/hqk,khe->qhe/dot_general | solution.py:34
  213.2 6.6 %copy_dynamic-update-slice_fusion.2 = f32[2,512,16,128]{3,2,1,0:T(8,128)} fusion(f32[2,512,16,128]{3,2,1,0:T(8,128)} %get-tuple-element.155, s32[]{:T(128)S(6)} %copy.194, f32[1,512,16,128]{3,1,2,0:T(8,128)} %fusion.68), kind=kLoop, calls=%fused_computation.13.clone.1 | loop fusion | bytes 8388612 | tf_op jit(solution)/shard_map/while/body/jit(dynamic_update_index_in_dim)/dynamic_update_slice | solution.py:110
  220.0 9.0 %copy.85 = bf16[8,128,16,128]{3,0,2,1:T(8,128)(2,1)} copy(bf16[8,128,16,128]{3,2,1,0:T(8,128)(2,1)} %bitcast.203) | data formatting | bytes 8388608 | tf_op jit(solution)/shard_map/reshape;reshape | solution.py:69
  232.2 6.9 %copy.83 = bf16[64,16,16,128]{3,0,2,1:T(8,128)(2,1)} copy(bf16[64,16,16,128]{3,2,1,0:T(8,128)(2,1)} %bitcast.204) | data formatting | bytes 8388608 | tf_op jit(solution)/shard_map/reshape;reshape | solution.py:69
  250.2 4.8 fusion.26
  255.4 128.8 %all-gather.6.cloned.1.call-done = bf16[1024,16,128]{2,0,1:T(8,128)(2,1)} async-done(((bf16[8,16,128]{2,0,1:T(8,128)(2,1)}), bf16[1024,16,128]{2,0,1:T(8,128)(2,1)}) %all-gather.6.cloned.1.call-update) | async-done | bytes 4194320 | tf_op jit(solution)/shard_map/all_gather | solution.py:127
  392.2 5.9 %div.11 = f32[1024,16,128]{2,1,0:T(8,128)} broadcast(f32[1024,16]{1,0:T(8,128)S(1)} %copy.98), dimensions={0,1} | broadcast | bytes 8454144 | tf_op jit(solution)/shard_map/div | solution.py:96
  398.1 6.0 %mul.91 = f32[1024,16,128]{2,1,0:T(8,128)} broadcast(f32[1024,16]{1,0:T(8,128)S(1)} %copy.96), dimensions={0,1} | broadcast | bytes 8454144 | tf_op jit(solution)/shard_map/mul | solution.py:95
  404.1 3.8 broadcast_in_dim.234
  407.9 6.0 %mul.87 = f32[1024,16,128]{2,1,0:T(8,128)} broadcast(f32[1024,16]{1,0:T(8,128)S(1)} %copy.91), dimensions={0,1} | broadcast | bytes 8454144 | tf_op jit(solution)/shard_map/mul | solution.py:95
  413.9 3.9 broadcast_in_dim.225
  417.8 5.8 %mul.83 = f32[1024,16,128]{2,1,0:T(8,128)} broadcast(f32[1024,16]{1,0:T(8,128)S(1)} %copy.87), dimensions={0,1} | broadcast | bytes 8454144 | tf_op jit(solution)/shard_map/mul | solution.py:95
  423.6 6.9 %broadcast_in_dim.228 = pred[1024,16,128]{2,1,0:T(8,128)(4,1)S(1)} broadcast(pred[1024,16]{1,0:T(8,128)(4,1)S(1)} %copy.92), dimensions={0,1} | broadcast | bytes 2113536 | tf_op jit(solution)/shard_map/jit(_where)/broadcast_in_dim | solution.py:80
  430.5 6.9 %broadcast_in_dim.219 = pred[1024,16,128]{2,1,0:T(8,128)(4,1)S(1)} broadcast(pred[1024,16]{1,0:T(8,128)(4,1)S(1)} %copy.88), dimensions={0,1} | broadcast | bytes 2113536 | tf_op jit(solution)/shard_map/jit(_where)/broadcast_in_dim | solution.py:80
  437.4 45.3 %fusion.11 = bf16[1024,2048]{1,0:T(8,128)(2,1)} fusion(f32[128,8,16,128]{3,2,1,0:T(8,128)} %bitcast.209, f32[128,8,16,128]{3,2,1,0:T(8,128)} %bitcast.210, f32[128,8,16,128]{3,2,1,0:T(8,128)} %bitcast.211, f32[128,8,16,128]{3,2,1,0:T(8,128)} %bitcast.212, f32[128,8,16,128]{3,2,1,0:T(8,128)} %bitcast.213, f32[128,8,16,128]{3,2,1,0:T(8,128)} %bitcast.214, ...), kind=kLoop, calls=%fused_computation.20 | loop fusion | flops 18874368 | bytes 67108864 | tf_op jit(solution)/shard_map/convert_element_type | solution.py:144
  (83 shorter events, 58.1 us)
Async XLA Ops:
  6.5 236.0 %all-gather.4.cloned.1.call-start = ((), (), s32[]{:S(2)}) async-start(), calls=%async_computation.1 | async-start | bytes 4456448 | tf_op jit(solution)/shard_map/all_gather | solution.py:133
  6.5 24.2 %copy-start.4 = (s32[16]{0:T(128)}, s32[16]{0:T(128)S(1)}, u32[]{:S(2)}) copy-start(s32[16]{0:T(128)S(1)} %fusion.48) | copy-start | bytes 196
  10.1 2.0 copy-start.2
  20.3 229.9 %all-gather.8.cloned.1.call-start = ((), (), s32[]{:S(2)}) async-start(), calls=%async_computation.3 | async-start | bytes 4456448 | tf_op jit(solution)/shard_map/all_gather | solution.py:134
  24.2 2.0 copy-start.3
  43.4 27.3 %copy-start.6 = (s32[16]{0:T(128)}, s32[16]{0:T(128)S(1)}, u32[]{:S(2)}) copy-start(s32[16]{0:T(128)S(1)} %fusion.50) | copy-start | bytes 196
  49.2 339.4 %all-to-all-start = ((bf16[128,8,16,128]{3,1,2,0:T(8,128)(2,1)}), bf16[128,8,16,128]{3,1,2,0:T(8,128)(2,1)}, u32[]{:S(2)}, u32[]{:S(2)}) async-start(bf16[128,8,16,128]{3,1,2,0:T(8,128)(2,1)} %stack.2), calls=%async_computation | async-start | bytes 8388608 | tf_op jit(solution)/shard_map/all_to_all | solution.py:17
  61.3 322.9 %all-gather.6.cloned.1.call-start = ((), (), s32[]{:S(2)}) async-start(), calls=%async_computation.2 | async-start | bytes 4227072 | tf_op jit(solution)/shard_map/all_gather | solution.py:127
  105.8 3.5 copy-start
  162.8 3.4 copy-start
  219.9 9.0 %copy-start.7 = (s32[16]{0:T(128)S(1)}, s32[16]{0:T(128)}, u32[]{:S(2)}) copy-start(s32[16]{0:T(128)} %copy-done.6) | copy-start | bytes 196
  219.9 11.8 %copy-start.8 = (pred[16,16]{0,1:T(8,128)(4,1)S(1)}, pred[16,16]{0,1:T(8,128)(4,1)}, u32[]{:S(2)}) copy-start(pred[16,16]{0,1:T(8,128)(4,1)} %constant.15.clone) | copy-start | bytes 772
  232.2 6.9 %copy-start.5 = (s32[16]{0:T(128)S(1)}, s32[16]{0:T(128)}, u32[]{:S(2)}) copy-start(s32[16]{0:T(128)} %copy-done.4) | copy-start | bytes 196
  232.2 9.7 %copy-start.9 = (pred[128,16]{0,1:T(8,128)(4,1)S(1)}, pred[128,16]{0,1:T(8,128)(4,1)}, u32[]{:S(2)}) copy-start(pred[128,16]{0,1:T(8,128)(4,1)} %constant.17.clone) | copy-start | bytes 6148
  246.4 2.0 copy-start.1
Sparse Core Ops, SparseCore 0:
  20.4 96.9 all-gather.3
  119.9 57.2 all-gather.7
  178.8 205.3 all-gather.5
